TPU v7x, 512 devices: a whole 4x4x16 slice. The times are simulated.
512 devices in a mesh: ctx: 32 (over z, core), ch: 16 (over x, y).
Axes of the slice: x: 4, y: 4, z: 16, core: 2. Of those that a mesh axis runs over, the one named last changes fastest.
Arguments:
- signal: bfloat16 [4096, 8192], P('ctx', 'ch'), may hold values from -170 to 170, as said below
- norm_gain: float32 [8192], P('ch'), may hold values from 0.1 to 1.9
- skip_gain: float32 [8192], P('ch'), may hold values from 0.5 to 1.5
- filter_taps: bfloat16 [4096, 8192], P('ctx', 'ch'), may hold values from -1.5 to 1.5, as said below
- out_gate: bfloat16 [4096, 8192], P('ctx', 'ch'), may hold values from -6 to 6
Outputs:
- mixture: bfloat16 [4096, 8192], P('ctx', 'ch')
Inputs may be any that keep to these rules, and one draw needn't show every extreme that they name: `signal`: features whose channels and tokens have different scales. `filter_taps`: a filter whose taps fall off along the lags at a rate that differs between channels.
All inputs are finite; a program needn't handle non-finite values.
Results may differ from a plain program's by a relative error of at most 0.006.
Values may be sent and summed in bfloat16 or wider, within the bound.
A program may use at most 64 MiB of HBM per device.

v0:
```python
import math

import jax
import jax.numpy as jnp
from jax import lax
from jax.sharding import PartitionSpec as P

C = 8192


EPS = 1e-06


def passed_along(block, axis, distance):
    devices = range(lax.axis_size(axis))
    route = [(i - distance, i) for i in devices if i - distance in devices]
    return lax.ppermute(block, axis, route)


def split_parts(matrix):
    high = matrix.astype(jnp.bfloat16)
    kept = lax.optimization_barrier(high)
    low = (matrix - kept.astype(jnp.float32)).astype(jnp.bfloat16)
    return (high, low)


def table_dot(table_pair, data):
    return jnp.dot(table_pair[0], data, preferred_element_type=jnp.float32) + jnp.dot(
        table_pair[1], data, preferred_element_type=jnp.float32
    )


def fine_dot(table_pair, data):
    data_high, data_low = split_parts(data)
    return (
        jnp.dot(table_pair[0], data_high, preferred_element_type=jnp.float32)
        + jnp.dot(table_pair[0], data_low, preferred_element_type=jnp.float32)
        + jnp.dot(table_pair[1], data_high, preferred_element_type=jnp.float32)
    )


def dft_tables(tok_rows):
    freq_ids = jnp.arange(tok_rows + 1, dtype=jnp.int32)
    row_ids = jnp.arange(tok_rows, dtype=jnp.int32)
    out_ids = jnp.arange(2 * tok_rows, dtype=jnp.int32)
    fwd_phase = (freq_ids[:, None] * row_ids[None, :] % (2 * tok_rows)).astype(jnp.float32) * (
        math.pi / tok_rows
    )
    inv_phase = (out_ids[:, None] * freq_ids[None, :] % (2 * tok_rows)).astype(jnp.float32) * (
        math.pi / tok_rows
    )
    weights = jnp.where((freq_ids == 0) | (freq_ids == tok_rows), 1.0, 2.0).astype(jnp.float32) / (
        2.0 * tok_rows
    )
    return (
        jnp.cos(fwd_phase),
        jnp.sin(fwd_phase),
        jnp.cos(inv_phase) * weights[None, :],
        jnp.sin(inv_phase) * weights[None, :],
    )


def local(signal, norm_gain, skip_gain, filter_taps, out_gate):
    tok_rows, channels = signal.shape
    ctx_count = lax.axis_size("ctx")
    ctx_index = lax.axis_index("ctx")
    values = signal.astype(jnp.float32)
    row_power = lax.psum(jnp.sum(values * values, axis=1), "ch") / C
    normed = (values * lax.rsqrt(row_power + EPS)[:, None] * norm_gain[None, :]).astype(
        jnp.bfloat16
    )
    fwd_cos, fwd_sin, inv_cos, inv_sin = dft_tables(tok_rows)
    cos_high, cos_low = split_parts(fwd_cos)
    sin_high, sin_low = split_parts(fwd_sin)
    halfway = ctx_count // 2
    quarter = ctx_count // 4
    helper = jnp.zeros((), jnp.bool_)
    first_own = jnp.zeros((), jnp.int32)
    partner = ctx_index + halfway
    whole_filter = lax.all_gather(filter_taps, "ctx", axis=0, tiled=True)

    def spectrum(segment):
        span_rows = segment.shape[0]
        cos_pair = (cos_high, cos_low)
        sin_pair = (sin_high, sin_low)
        return (table_dot(cos_pair, segment), -table_dot(sin_pair, segment))

    def lag_product(lag_block, sig_re, sig_im, sum_re, sum_im):
        taps = lax.dynamic_slice_in_dim(whole_filter, lag_block * tok_rows, tok_rows, 0)
        fil_re, fil_im = spectrum(taps)
        return (
            sum_re + fil_re * sig_re - fil_im * sig_im,
            sum_im + fil_re * sig_im + fil_im * sig_re,
        )

    blank = jnp.zeros((tok_rows + 1, channels), jnp.float32)
    segment_in = lax.all_gather(normed, "ctx", axis=0, tiled=True)
    span_rows = min(segment_in.shape[0], tok_rows)

    def one_span(sub_index, running):
        anchor = sub_index * span_rows
        segment = lax.dynamic_slice_in_dim(segment_in, sub_index * span_rows, span_rows, 0)
        source = anchor // tok_rows
        own_ok = (source <= ctx_index) & (source >= first_own)
        help_ok = helper & (source < quarter)

        def do_work(state):
            sig_re, sig_im = spectrum(segment)

            def own_add(pair_in):
                return lag_product(ctx_index - source, sig_re, sig_im, pair_in[0], pair_in[1])

            def help_add(pair_in):
                return lag_product(partner - source, sig_re, sig_im, pair_in[0], pair_in[1])

            def keep_pair(pair_in):
                return pair_in

            own_re, own_im = lax.cond(own_ok, own_add, keep_pair, (state[0], state[1]))
            help_re, help_im = lax.cond(help_ok, help_add, keep_pair, (state[2], state[3]))
            return (own_re, own_im, help_re, help_im)

        def skip_work(state):
            return state

        return lax.cond(own_ok | help_ok, do_work, skip_work, running)

    own_re, own_im, help_re, help_im = lax.fori_loop(
        0, segment_in.shape[0] // span_rows, one_span, (blank, blank, blank, blank)
    )
    low_cos = split_parts(inv_cos[:tok_rows])
    low_sin = split_parts(inv_sin[:tok_rows])
    high_cos = split_parts(inv_cos[tok_rows:])
    high_sin = split_parts(inv_sin[tok_rows:])
    low_part = fine_dot(low_cos, own_re) - fine_dot(low_sin, own_im)
    high_part = fine_dot(high_cos, own_re) - fine_dot(high_sin, own_im)
    convolved = low_part + passed_along(high_part.astype(jnp.bfloat16), "ctx", 1).astype(
        high_part.dtype
    )
    mixture = out_gate.astype(jnp.float32) * (
        convolved + skip_gain[None, :] * normed.astype(jnp.float32)
    )
    return mixture.astype(jnp.bfloat16)


def solution(mesh):
    return jax.shard_map(
        local,
        mesh=mesh,
        in_specs=(P("ctx", "ch"), P("ch"), P("ch"), P("ctx", "ch"), P("ctx", "ch")),
        out_specs=P("ctx", "ch"),
        check_vma=False,
    )
```

profile of v0, /device:TPU:487, one launch (start us, length us, event | category | flops | bytes accessed | tf_op | source)
XLA Modules:
  0.0 462.1 jit_solution(6223332939443053521)
XLA Ops:
  8.3 27.3 %psum.7 = f32[128]{0:T(128)S(1)} all-reduce(f32[128]{0:T(128)S(1)} %fusion.33), channel_id=1, replica_groups=mesh['ctx'=32,'ch'=16] {'ch'}, use_global_device_ids=true, to_apply=%region_1.0 | all-reduce | flops 128 | bytes 1024 | tf_op jit(solution)/shard_map/psum | solution.py:68
  39.3 42.0 %all-gather.5.cloned.1.call-done = bf16[4096,512]{1,0:T(8,128)(2,1)} async-done(((bf16[128,512]{1,0:T(8,128)(2,1)}), bf16[4096,512]{1,0:T(8,128)(2,1)}) %all-gather.5.cloned.1.call-update) | async-done | bytes 4194320 | tf_op jit(solution)/shard_map/all_gather | solution.py:80
  81.3 73.2 %all-gather.3.cloned.1.call-done = bf16[4096,512]{1,0:T(8,128)(2,1)} async-done(((bf16[128,512]{1,0:T(8,128)(2,1)}), bf16[4096,512]{1,0:T(8,128)(2,1)}) %all-gather.3.cloned.1.call-update) | async-done | bytes 4194320 | tf_op jit(solution)/shard_map/all_gather | solution.py:97
  154.6 294.8 %while.19 = (s32[]{:T(128)}, f32[129,512]{1,0:T(8,128)S(1)}, f32[129,512]{1,0:T(8,128)S(1)}, s32[]{:T(128)}, bf16[4096,512]{1,0:T(8,128)(2,1)}, /*index=5*/bf16[...) while((s32[]{:T(128)}, f32[129,512]{1,0:T(8,128)S(1)}, ...), condition=%wide.region_7.8_spmd.clone.clone, body=%wide.region_2.7_spmd.clone.clone.sunk | while | flops 136455184 | bytes 6134993 | solution.py:128
  164.1 8.9 %conditional.5 = ((f32[129,512]{1,0:T(8,128)S(1)}, f32[129,512]{1,0:T(8,128)S(1)})) conditional(s32[]{:T(128)} %convert_element_type.331, (f32[129,512]{1,0:T(8,128)S(1)}, f32[129,512]{1,0:T(8,128)S(1)}) %tuple.76, (pred[]{:T(512)}, s32[]{:T(128)}, pred[]{:T(512)}, bf16[4096,512]{1,0:T(8,128)(2,1)}, bf16[129,128]{1,0:T(8,128)(2,1)S(1)}, ...), branch_computations={%region_3.3_spmd, %region_4.6_spmd} | conditional | flops 136190976 | bytes 6068488 | solution.py:126
  173.4 8.9 %conditional.5 = ((f32[129,512]{1,0:T(8,128)S(1)}, f32[129,512]{1,0:T(8,128)S(1)})) conditional(s32[]{:T(128)} %convert_element_type.331, (f32[129,512]{1,0:T(8,128)S(1)}, f32[129,512]{1,0:T(8,128)S(1)}) %tuple.76, (pred[]{:T(512)}, s32[]{:T(128)}, pred[]{:T(512)}, bf16[4096,512]{1,0:T(8,128)(2,1)}, bf16[129,128]{1,0:T(8,128)(2,1)S(1)}, ...), branch_computations={%region_3.3_spmd, %region_4.6_spmd} | conditional | flops 136190976 | bytes 6068488 | solution.py:126
  182.6 8.9 %conditional.5 = ((f32[129,512]{1,0:T(8,128)S(1)}, f32[129,512]{1,0:T(8,128)S(1)})) conditional(s32[]{:T(128)} %convert_element_type.331, (f32[129,512]{1,0:T(8,128)S(1)}, f32[129,512]{1,0:T(8,128)S(1)}) %tuple.76, (pred[]{:T(512)}, s32[]{:T(128)}, pred[]{:T(512)}, bf16[4096,512]{1,0:T(8,128)(2,1)}, bf16[129,128]{1,0:T(8,128)(2,1)S(1)}, ...), branch_computations={%region_3.3_spmd, %region_4.6_spmd} | conditional | flops 136190976 | bytes 6068488 | solution.py:126
  191.8 8.9 %conditional.5 = ((f32[129,512]{1,0:T(8,128)S(1)}, f32[129,512]{1,0:T(8,128)S(1)})) conditional(s32[]{:T(128)} %convert_element_type.331, (f32[129,512]{1,0:T(8,128)S(1)}, f32[129,512]{1,0:T(8,128)S(1)}) %tuple.76, (pred[]{:T(512)}, s32[]{:T(128)}, pred[]{:T(512)}, bf16[4096,512]{1,0:T(8,128)(2,1)}, bf16[129,128]{1,0:T(8,128)(2,1)S(1)}, ...), branch_computations={%region_3.3_spmd, %region_4.6_spmd} | conditional | flops 136190976 | bytes 6068488 | solution.py:126
  201.0 8.9 %conditional.5 = ((f32[129,512]{1,0:T(8,128)S(1)}, f32[129,512]{1,0:T(8,128)S(1)})) conditional(s32[]{:T(128)} %convert_element_type.331, (f32[129,512]{1,0:T(8,128)S(1)}, f32[129,512]{1,0:T(8,128)S(1)}) %tuple.76, (pred[]{:T(512)}, s32[]{:T(128)}, pred[]{:T(512)}, bf16[4096,512]{1,0:T(8,128)(2,1)}, bf16[129,128]{1,0:T(8,128)(2,1)S(1)}, ...), branch_computations={%region_3.3_spmd, %region_4.6_spmd} | conditional | flops 136190976 | bytes 6068488 | solution.py:126
  210.2 8.9 %conditional.5 = ((f32[129,512]{1,0:T(8,128)S(1)}, f32[129,512]{1,0:T(8,128)S(1)})) conditional(s32[]{:T(128)} %convert_element_type.331, (f32[129,512]{1,0:T(8,128)S(1)}, f32[129,512]{1,0:T(8,128)S(1)}) %tuple.76, (pred[]{:T(512)}, s32[]{:T(128)}, pred[]{:T(512)}, bf16[4096,512]{1,0:T(8,128)(2,1)}, bf16[129,128]{1,0:T(8,128)(2,1)S(1)}, ...), branch_computations={%region_3.3_spmd, %region_4.6_spmd} | conditional | flops 136190976 | bytes 6068488 | solution.py:126
  219.4 8.9 %conditional.5 = ((f32[129,512]{1,0:T(8,128)S(1)}, f32[129,512]{1,0:T(8,128)S(1)})) conditional(s32[]{:T(128)} %convert_element_type.331, (f32[129,512]{1,0:T(8,128)S(1)}, f32[129,512]{1,0:T(8,128)S(1)}) %tuple.76, (pred[]{:T(512)}, s32[]{:T(128)}, pred[]{:T(512)}, bf16[4096,512]{1,0:T(8,128)(2,1)}, bf16[129,128]{1,0:T(8,128)(2,1)S(1)}, ...), branch_computations={%region_3.3_spmd, %region_4.6_spmd} | conditional | flops 136190976 | bytes 6068488 | solution.py:126
  228.6 8.9 %conditional.5 = ((f32[129,512]{1,0:T(8,128)S(1)}, f32[129,512]{1,0:T(8,128)S(1)})) conditional(s32[]{:T(128)} %convert_element_type.331, (f32[129,512]{1,0:T(8,128)S(1)}, f32[129,512]{1,0:T(8,128)S(1)}) %tuple.76, (pred[]{:T(512)}, s32[]{:T(128)}, pred[]{:T(512)}, bf16[4096,512]{1,0:T(8,128)(2,1)}, bf16[129,128]{1,0:T(8,128)(2,1)S(1)}, ...), branch_computations={%region_3.3_spmd, %region_4.6_spmd} | conditional | flops 136190976 | bytes 6068488 | solution.py:126
  237.8 8.9 %conditional.5 = ((f32[129,512]{1,0:T(8,128)S(1)}, f32[129,512]{1,0:T(8,128)S(1)})) conditional(s32[]{:T(128)} %convert_element_type.331, (f32[129,512]{1,0:T(8,128)S(1)}, f32[129,512]{1,0:T(8,128)S(1)}) %tuple.76, (pred[]{:T(512)}, s32[]{:T(128)}, pred[]{:T(512)}, bf16[4096,512]{1,0:T(8,128)(2,1)}, bf16[129,128]{1,0:T(8,128)(2,1)S(1)}, ...), branch_computations={%region_3.3_spmd, %region_4.6_spmd} | conditional | flops 136190976 | bytes 6068488 | solution.py:126
  247.1 8.9 %conditional.5 = ((f32[129,512]{1,0:T(8,128)S(1)}, f32[129,512]{1,0:T(8,128)S(1)})) conditional(s32[]{:T(128)} %convert_element_type.331, (f32[129,512]{1,0:T(8,128)S(1)}, f32[129,512]{1,0:T(8,128)S(1)}) %tuple.76, (pred[]{:T(512)}, s32[]{:T(128)}, pred[]{:T(512)}, bf16[4096,512]{1,0:T(8,128)(2,1)}, bf16[129,128]{1,0:T(8,128)(2,1)S(1)}, ...), branch_computations={%region_3.3_spmd, %region_4.6_spmd} | conditional | flops 136190976 | bytes 6068488 | solution.py:126
  256.3 8.9 %conditional.5 = ((f32[129,512]{1,0:T(8,128)S(1)}, f32[129,512]{1,0:T(8,128)S(1)})) conditional(s32[]{:T(128)} %convert_element_type.331, (f32[129,512]{1,0:T(8,128)S(1)}, f32[129,512]{1,0:T(8,128)S(1)}) %tuple.76, (pred[]{:T(512)}, s32[]{:T(128)}, pred[]{:T(512)}, bf16[4096,512]{1,0:T(8,128)(2,1)}, bf16[129,128]{1,0:T(8,128)(2,1)S(1)}, ...), branch_computations={%region_3.3_spmd, %region_4.6_spmd} | conditional | flops 136190976 | bytes 6068488 | solution.py:126
  265.5 8.9 %conditional.5 = ((f32[129,512]{1,0:T(8,128)S(1)}, f32[129,512]{1,0:T(8,128)S(1)})) conditional(s32[]{:T(128)} %convert_element_type.331, (f32[129,512]{1,0:T(8,128)S(1)}, f32[129,512]{1,0:T(8,128)S(1)}) %tuple.76, (pred[]{:T(512)}, s32[]{:T(128)}, pred[]{:T(512)}, bf16[4096,512]{1,0:T(8,128)(2,1)}, bf16[129,128]{1,0:T(8,128)(2,1)S(1)}, ...), branch_computations={%region_3.3_spmd, %region_4.6_spmd} | conditional | flops 136190976 | bytes 6068488 | solution.py:126
  274.7 8.9 %conditional.5 = ((f32[129,512]{1,0:T(8,128)S(1)}, f32[129,512]{1,0:T(8,128)S(1)})) conditional(s32[]{:T(128)} %convert_element_type.331, (f32[129,512]{1,0:T(8,128)S(1)}, f32[129,512]{1,0:T(8,128)S(1)}) %tuple.76, (pred[]{:T(512)}, s32[]{:T(128)}, pred[]{:T(512)}, bf16[4096,512]{1,0:T(8,128)(2,1)}, bf16[129,128]{1,0:T(8,128)(2,1)S(1)}, ...), branch_computations={%region_3.3_spmd, %region_4.6_spmd} | conditional | flops 136190976 | bytes 6068488 | solution.py:126
  283.9 8.9 %conditional.5 = ((f32[129,512]{1,0:T(8,128)S(1)}, f32[129,512]{1,0:T(8,128)S(1)})) conditional(s32[]{:T(128)} %convert_element_type.331, (f32[129,512]{1,0:T(8,128)S(1)}, f32[129,512]{1,0:T(8,128)S(1)}) %tuple.76, (pred[]{:T(512)}, s32[]{:T(128)}, pred[]{:T(512)}, bf16[4096,512]{1,0:T(8,128)(2,1)}, bf16[129,128]{1,0:T(8,128)(2,1)S(1)}, ...), branch_computations={%region_3.3_spmd, %region_4.6_spmd} | conditional | flops 136190976 | bytes 6068488 | solution.py:126
  293.1 8.9 %conditional.5 = ((f32[129,512]{1,0:T(8,128)S(1)}, f32[129,512]{1,0:T(8,128)S(1)})) conditional(s32[]{:T(128)} %convert_element_type.331, (f32[129,512]{1,0:T(8,128)S(1)}, f32[129,512]{1,0:T(8,128)S(1)}) %tuple.76, (pred[]{:T(512)}, s32[]{:T(128)}, pred[]{:T(512)}, bf16[4096,512]{1,0:T(8,128)(2,1)}, bf16[129,128]{1,0:T(8,128)(2,1)S(1)}, ...), branch_computations={%region_3.3_spmd, %region_4.6_spmd} | conditional | flops 136190976 | bytes 6068488 | solution.py:126
  302.3 8.9 %conditional.5 = ((f32[129,512]{1,0:T(8,128)S(1)}, f32[129,512]{1,0:T(8,128)S(1)})) conditional(s32[]{:T(128)} %convert_element_type.331, (f32[129,512]{1,0:T(8,128)S(1)}, f32[129,512]{1,0:T(8,128)S(1)}) %tuple.76, (pred[]{:T(512)}, s32[]{:T(128)}, pred[]{:T(512)}, bf16[4096,512]{1,0:T(8,128)(2,1)}, bf16[129,128]{1,0:T(8,128)(2,1)S(1)}, ...), branch_computations={%region_3.3_spmd, %region_4.6_spmd} | conditional | flops 136190976 | bytes 6068488 | solution.py:126
  311.6 8.9 %conditional.5 = ((f32[129,512]{1,0:T(8,128)S(1)}, f32[129,512]{1,0:T(8,128)S(1)})) conditional(s32[]{:T(128)} %convert_element_type.331, (f32[129,512]{1,0:T(8,128)S(1)}, f32[129,512]{1,0:T(8,128)S(1)}) %tuple.76, (pred[]{:T(512)}, s32[]{:T(128)}, pred[]{:T(512)}, bf16[4096,512]{1,0:T(8,128)(2,1)}, bf16[129,128]{1,0:T(8,128)(2,1)S(1)}, ...), branch_computations={%region_3.3_spmd, %region_4.6_spmd} | conditional | flops 136190976 | bytes 6068488 | solution.py:126
  320.8 8.9 %conditional.5 = ((f32[129,512]{1,0:T(8,128)S(1)}, f32[129,512]{1,0:T(8,128)S(1)})) conditional(s32[]{:T(128)} %convert_element_type.331, (f32[129,512]{1,0:T(8,128)S(1)}, f32[129,512]{1,0:T(8,128)S(1)}) %tuple.76, (pred[]{:T(512)}, s32[]{:T(128)}, pred[]{:T(512)}, bf16[4096,512]{1,0:T(8,128)(2,1)}, bf16[129,128]{1,0:T(8,128)(2,1)S(1)}, ...), branch_computations={%region_3.3_spmd, %region_4.6_spmd} | conditional | flops 136190976 | bytes 6068488 | solution.py:126
  330.0 8.9 %conditional.5 = ((f32[129,512]{1,0:T(8,128)S(1)}, f32[129,512]{1,0:T(8,128)S(1)})) conditional(s32[]{:T(128)} %convert_element_type.331, (f32[129,512]{1,0:T(8,128)S(1)}, f32[129,512]{1,0:T(8,128)S(1)}) %tuple.76, (pred[]{:T(512)}, s32[]{:T(128)}, pred[]{:T(512)}, bf16[4096,512]{1,0:T(8,128)(2,1)}, bf16[129,128]{1,0:T(8,128)(2,1)S(1)}, ...), branch_computations={%region_3.3_spmd, %region_4.6_spmd} | conditional | flops 136190976 | bytes 6068488 | solution.py:126
  339.2 8.9 %conditional.5 = ((f32[129,512]{1,0:T(8,128)S(1)}, f32[129,512]{1,0:T(8,128)S(1)})) conditional(s32[]{:T(128)} %convert_element_type.331, (f32[129,512]{1,0:T(8,128)S(1)}, f32[129,512]{1,0:T(8,128)S(1)}) %tuple.76, (pred[]{:T(512)}, s32[]{:T(128)}, pred[]{:T(512)}, bf16[4096,512]{1,0:T(8,128)(2,1)}, bf16[129,128]{1,0:T(8,128)(2,1)S(1)}, ...), branch_computations={%region_3.3_spmd, %region_4.6_spmd} | conditional | flops 136190976 | bytes 6068488 | solution.py:126
  348.4 8.9 %conditional.5 = ((f32[129,512]{1,0:T(8,128)S(1)}, f32[129,512]{1,0:T(8,128)S(1)})) conditional(s32[]{:T(128)} %convert_element_type.331, (f32[129,512]{1,0:T(8,128)S(1)}, f32[129,512]{1,0:T(8,128)S(1)}) %tuple.76, (pred[]{:T(512)}, s32[]{:T(128)}, pred[]{:T(512)}, bf16[4096,512]{1,0:T(8,128)(2,1)}, bf16[129,128]{1,0:T(8,128)(2,1)S(1)}, ...), branch_computations={%region_3.3_spmd, %region_4.6_spmd} | conditional | flops 136190976 | bytes 6068488 | solution.py:126
  357.6 8.9 %conditional.5 = ((f32[129,512]{1,0:T(8,128)S(1)}, f32[129,512]{1,0:T(8,128)S(1)})) conditional(s32[]{:T(128)} %convert_element_type.331, (f32[129,512]{1,0:T(8,128)S(1)}, f32[129,512]{1,0:T(8,128)S(1)}) %tuple.76, (pred[]{:T(512)}, s32[]{:T(128)}, pred[]{:T(512)}, bf16[4096,512]{1,0:T(8,128)(2,1)}, bf16[129,128]{1,0:T(8,128)(2,1)S(1)}, ...), branch_computations={%region_3.3_spmd, %region_4.6_spmd} | conditional | flops 136190976 | bytes 6068488 | solution.py:126
  366.8 8.9 %conditional.5 = ((f32[129,512]{1,0:T(8,128)S(1)}, f32[129,512]{1,0:T(8,128)S(1)})) conditional(s32[]{:T(128)} %convert_element_type.331, (f32[129,512]{1,0:T(8,128)S(1)}, f32[129,512]{1,0:T(8,128)S(1)}) %tuple.76, (pred[]{:T(512)}, s32[]{:T(128)}, pred[]{:T(512)}, bf16[4096,512]{1,0:T(8,128)(2,1)}, bf16[129,128]{1,0:T(8,128)(2,1)S(1)}, ...), branch_computations={%region_3.3_spmd, %region_4.6_spmd} | conditional | flops 136190976 | bytes 6068488 | solution.py:126
  376.0 8.9 %conditional.5 = ((f32[129,512]{1,0:T(8,128)S(1)}, f32[129,512]{1,0:T(8,128)S(1)})) conditional(s32[]{:T(128)} %convert_element_type.331, (f32[129,512]{1,0:T(8,128)S(1)}, f32[129,512]{1,0:T(8,128)S(1)}) %tuple.76, (pred[]{:T(512)}, s32[]{:T(128)}, pred[]{:T(512)}, bf16[4096,512]{1,0:T(8,128)(2,1)}, bf16[129,128]{1,0:T(8,128)(2,1)S(1)}, ...), branch_computations={%region_3.3_spmd, %region_4.6_spmd} | conditional | flops 136190976 | bytes 6068488 | solution.py:126
  385.3 8.9 %conditional.5 = ((f32[129,512]{1,0:T(8,128)S(1)}, f32[129,512]{1,0:T(8,128)S(1)})) conditional(s32[]{:T(128)} %convert_element_type.331, (f32[129,512]{1,0:T(8,128)S(1)}, f32[129,512]{1,0:T(8,128)S(1)}) %tuple.76, (pred[]{:T(512)}, s32[]{:T(128)}, pred[]{:T(512)}, bf16[4096,512]{1,0:T(8,128)(2,1)}, bf16[129,128]{1,0:T(8,128)(2,1)S(1)}, ...), branch_computations={%region_3.3_spmd, %region_4.6_spmd} | conditional | flops 136190976 | bytes 6068488 | solution.py:126
  394.5 8.9 %conditional.5 = ((f32[129,512]{1,0:T(8,128)S(1)}, f32[129,512]{1,0:T(8,128)S(1)})) conditional(s32[]{:T(128)} %convert_element_type.331, (f32[129,512]{1,0:T(8,128)S(1)}, f32[129,512]{1,0:T(8,128)S(1)}) %tuple.76, (pred[]{:T(512)}, s32[]{:T(128)}, pred[]{:T(512)}, bf16[4096,512]{1,0:T(8,128)(2,1)}, bf16[129,128]{1,0:T(8,128)(2,1)S(1)}, ...), branch_computations={%region_3.3_spmd, %region_4.6_spmd} | conditional | flops 136190976 | bytes 6068488 | solution.py:126
  403.7 8.9 %conditional.5 = ((f32[129,512]{1,0:T(8,128)S(1)}, f32[129,512]{1,0:T(8,128)S(1)})) conditional(s32[]{:T(128)} %convert_element_type.331, (f32[129,512]{1,0:T(8,128)S(1)}, f32[129,512]{1,0:T(8,128)S(1)}) %tuple.76, (pred[]{:T(512)}, s32[]{:T(128)}, pred[]{:T(512)}, bf16[4096,512]{1,0:T(8,128)(2,1)}, bf16[129,128]{1,0:T(8,128)(2,1)S(1)}, ...), branch_computations={%region_3.3_spmd, %region_4.6_spmd} | conditional | flops 136190976 | bytes 6068488 | solution.py:126
  440.5 8.9 %conditional.5 = ((f32[129,512]{1,0:T(8,128)S(1)}, f32[129,512]{1,0:T(8,128)S(1)})) conditional(s32[]{:T(128)} %convert_element_type.331, (f32[129,512]{1,0:T(8,128)S(1)}, f32[129,512]{1,0:T(8,128)S(1)}) %tuple.76, (pred[]{:T(512)}, s32[]{:T(128)}, pred[]{:T(512)}, bf16[4096,512]{1,0:T(8,128)(2,1)}, bf16[129,128]{1,0:T(8,128)(2,1)S(1)}, ...), branch_computations={%region_3.3_spmd, %region_4.6_spmd} | conditional | flops 136190976 | bytes 6068488 | solution.py:126
  (361 shorter events, 478.5 us)
Async XLA Ops:
  6.5 74.8 %all-gather.5.cloned.1.call-start = ((), (), s32[]{:S(2)}) async-start(), calls=%async_computation.1 | async-start | bytes 4325376 | tf_op jit(solution)/shard_map/all_gather | solution.py:80
  7.3 147.3 %all-gather.3.cloned.1.call-start = ((), (), s32[]{:S(2)}) async-start(), calls=%async_computation | async-start | bytes 4325376 | tf_op jit(solution)/shard_map/all_gather | solution.py:97
  449.6 4.8 %copy-start = (bf16[128,512]{1,0:T(8,128)(2,1)S(1)}, bf16[128,512]{1,0:T(8,128)(2,1)}, u32[]{:S(2)}) copy-start(bf16[128,512]{1,0:T(8,128)(2,1)} %fusion.35) | copy-start | bytes 393220
  449.6 4.8 %copy-start.1 = (bf16[128,512]{1,0:T(8,128)(2,1)S(1)}, bf16[128,512]{1,0:T(8,128)(2,1)}, u32[]{:S(2)}) copy-start(bf16[128,512]{1,0:T(8,128)(2,1)} %param.15) | copy-start | bytes 393220
  449.6 4.8 %copy-start.2 = (f32[512]{0:T(512)S(1)}, f32[512]{0:T(512)}, u32[]{:S(2)}) copy-start(f32[512]{0:T(512)} %param.13) | copy-start | bytes 6148
  451.1 3.2 collective-permute-start
Sparse Core Ops, SparseCore 0:
  9.5 71.7 all-gather.4
  83.4 71.0 all-gather.2
where the time goes:
time: 467 us; the launch traced here: 462 us
  matrix products  282 us (60%)
  waiting for transfers between devices  118 us (25%)
  blocking collectives  27.3 us (6%)
  other arithmetic  14.2 us (3%)
  between operations  13.6 us (3%)
  loops' own time  5.88 us (1%)
    dot_general x128, matrix products, table_dot(): jnp.dot(table_pair[1], data, preferred_element_type=jnp.float32)  141 us
    dot_general x128, matrix products, table_dot(): jnp.dot(table_pair[0], data, preferred_element_type=jnp.float32)  138 us
    all_gather x1, waiting for transfers between devices, local(): segment_in = lax.all_gather(normed, 'ctx', axis=0, tiled=True)  73.2 us
    all_gather x1, waiting for transfers between devices, local(): whole_filter = lax.all_gather(filter_taps, 'ctx', axis=0, tiled=True)  42 us
    psum x1, blocking collectives, local(): row_power = lax.psum(jnp.sum(values * values, axis=1), 'ch') / C  27.3 us
    convert_element_type x36, other arithmetic, split_parts(): high = matrix.astype(jnp.bfloat16)  10.1 us
  transfers between devices with their start and end apart: 3, of which 3 were waited for; matrix products, arithmetic and copies ran while one was open for 1% of the time, Pallas kernels for 0%

commit v1 on v0

v1 whole, which is shorter than its diff:
```python
import functools
import math

import jax
import jax.numpy as jnp
import ml_dtypes
import numpy as np
from jax import lax
from jax.experimental import pallas as pl
from jax.experimental.pallas import tpu as pltpu
from jax.sharding import PartitionSpec as P

C = 8192
EPS = 1e-06
MESH = pl.DeviceIdType.MESH
STEP = 4


def high_low(table):
    high = table.astype(ml_dtypes.bfloat16)
    low = (table - high.astype(np.float64)).astype(ml_dtypes.bfloat16)
    return high, low


def dft_tables(rows):
    span = 2 * rows
    freq = np.arange(rows)
    def phase(a, b):
        return (a[:, None] * b[None, :] % span) * (2.0 * math.pi / span)
    row = np.arange(rows)
    angle = phase(row, freq)
    fwd_im = -np.sin(angle)
    fwd_im[:, 0] = np.cos(math.pi * row)
    forward = np.concatenate([np.cos(angle), fwd_im], axis=1)
    out = np.arange(span)
    angle = phase(freq, out)
    inv_re = 2.0 * np.cos(angle) / span
    inv_re[0] = 1.0 / span
    inv_im = -2.0 * np.sin(angle) / span
    inv_im[0] = np.cos(math.pi * out) / span
    inverse = np.concatenate([inv_re, inv_im], axis=0)
    fwd = np.concatenate(high_low(forward), axis=0)
    inv = np.stack(high_low(inverse), axis=0)
    return fwd, inv


def kernel(
    n_ctx, n_ch, channels_all,
    sig_hbm, tap_hbm, gate_hbm, gain_ref, skip_ref, fwd_hbm, inv_hbm, out_ref,
    sig, tap, gate, fwd, inv, in_sem,
    outbox, inbox, send_sem, recv_sem,
    part, part_send, part_recv, power, power_send, power_recv,
    columns, normed, spec_x, spec_h, spec_y, tail,
    back_out, back_in, back_send, back_recv,
):
    rows, chans = sig.shape
    cpd = chans // n_ctx
    half = cpd // 2
    me = lax.axis_index("ctx")
    me_ch = lax.axis_index("ch")

    loads = [
        pltpu.make_async_copy(src, dst, in_sem.at[k])
        for k, (src, dst) in enumerate(
            ((sig_hbm, sig), (tap_hbm, tap), (fwd_hbm, fwd), (gate_hbm, gate), (inv_hbm, inv))
        )
    ]
    for load in loads:
        load.start()

    barrier = pltpu.get_barrier_semaphore()

    def greet_ctx(d, _):
        pl.semaphore_signal(barrier, inc=1, device_id={"ctx": lax.rem(me + d, n_ctx)}, device_id_type=MESH)
        return 0

    def greet_ch(d, _):
        pl.semaphore_signal(barrier, inc=1, device_id={"ch": lax.rem(me_ch + d, n_ch)}, device_id_type=MESH)
        return 0

    lax.fori_loop(1, n_ch, greet_ch, 0)
    lax.fori_loop(1, n_ctx, greet_ctx, 0)

    loads[0].wait()
    values = sig[...].astype(jnp.float32).T
    part[pl.ds(me_ch, 1)] = jnp.sum(values * values, axis=0, keepdims=True).reshape(1, 1, rows)
    outbox[:, 0] = values.astype(jnp.bfloat16).reshape(n_ctx, cpd, rows)
    loads[1].wait()
    outbox[:, 1] = tap[...].astype(jnp.float32).T.astype(jnp.bfloat16).reshape(n_ctx, cpd, rows)

    pl.semaphore_wait(barrier, n_ctx + n_ch - 2)

    def part_copy(peer, slot):
        return pltpu.make_async_remote_copy(
            src_ref=part.at[me_ch], dst_ref=part.at[slot], send_sem=part_send.at[peer], recv_sem=part_recv.at[slot],
            device_id={"ch": peer}, device_id_type=MESH,
        )

    def bulk_copy(peer, slot):
        return pltpu.make_async_remote_copy(
            src_ref=outbox.at[peer], dst_ref=inbox.at[slot], send_sem=send_sem.at[peer], recv_sem=recv_sem.at[slot],
            device_id={"ctx": peer}, device_id_type=MESH,
        )

    def power_copy(peer, slot):
        return pltpu.make_async_remote_copy(
            src_ref=power.at[me], dst_ref=power.at[slot], send_sem=power_send.at[peer], recv_sem=power_recv.at[slot],
            device_id={"ctx": peer}, device_id_type=MESH,
        )

    def back_copy(peer, slot):
        return pltpu.make_async_remote_copy(
            src_ref=back_out.at[peer], dst_ref=back_in.at[slot], send_sem=back_send.at[peer], recv_sem=back_recv.at[slot],
            device_id={"ctx": peer}, device_id_type=MESH,
        )

    def ctx_peer(n):
        far = n_ctx // 2 - n // 2
        return lax.rem(jnp.where(n % 2 == 0, me + far, me + n_ctx - far), n_ctx)

    def over_ctx(action):
        def step(n, _):
            action(ctx_peer(n))
            return 0
        lax.fori_loop(1, n_ctx, step, 0)

    def over_ch(action):
        def step(d, _):
            action(lax.rem(me_ch + d, n_ch))
            return 0
        lax.fori_loop(1, n_ch, step, 0)

    over_ch(lambda peer: part_copy(peer, me_ch).start())
    over_ctx(lambda peer: bulk_copy(peer, me).start())
    inbox[pl.ds(me, 1)] = outbox[pl.ds(me, 1)]

    first = me * cpd
    width = columns.shape[1]
    spot = pl.ds(pl.multiple_of(lax.rem(first, width), cpd), cpd)
    for k, ref in enumerate((gain_ref, skip_ref)):
        line = ref[pl.ds(first // width, 1), :]
        columns[k] = jnp.broadcast_to(line, (rows, width)).T
    gain = columns[0, spot, :]
    skip = columns[1, spot, :]

    over_ch(lambda peer: part_copy(peer, peer).wait_recv())
    total = jnp.sum(part[...], axis=0, keepdims=True)
    power[pl.ds(me, 1)] = lax.rsqrt(total / channels_all + EPS)
    over_ctx(lambda peer: power_copy(peer, me).start())

    lane = lax.broadcasted_iota(jnp.int32, (1, 1, rows), 2)
    spec_h[:, :STEP] = jnp.zeros((3, STEP, cpd, rows), jnp.float32)
    tail[...] = jnp.zeros_like(tail)
    over_ctx(lambda peer: power_copy(peer, peer).wait_recv())
    over_ctx(lambda peer: bulk_copy(peer, peer).wait_recv())
    loads[2].wait()

    def transform(n, _):
        at = pl.ds(pl.multiple_of(n * STEP, STEP), STEP)
        later = pl.ds(pl.multiple_of(n * STEP + STEP, STEP), STEP)
        features = inbox[at, 0].astype(jnp.float32)
        scaled = (features * power[at] * gain[None]).astype(jnp.bfloat16)
        normed[at] = scaled
        both = jnp.concatenate([scaled, inbox[at, 1]], axis=0).reshape(2 * STEP * cpd, rows)
        spectrum = jnp.dot(
            jnp.concatenate([both, both], axis=1), fwd[...], preferred_element_type=jnp.float32
        ).reshape(2, STEP, cpd, 2 * rows)
        spec_x[0, at] = spectrum[0, :, :, :rows]
        spec_x[1, at] = spectrum[0, :, :, rows:]
        h_re = spectrum[1, :, :, :rows]
        h_im = spectrum[1, :, :, rows:]
        spec_h[0, later] = h_re
        spec_h[1, later] = jnp.where(lane == 0, 0.0, h_im)
        spec_h[2, later] = jnp.where(lane == 0, h_im, h_re)
        return 0

    lax.fori_loop(0, n_ctx // STEP, transform, 0)

    def convolve(n, _):
        for part_no in range(2):
            sub = pl.ds(part_no * half, half)

            def add_blocks(m, sums):
                sums = list(sums)
                base = (n - m) * STEP
                for b in range(STEP):
                    x_re = spec_x[0, m * STEP + b, sub, :]
                    x_im = spec_x[1, m * STEP + b, sub, :]
                    for a in range(STEP):
                        k = base + a - b + STEP
                        h_re = spec_h[0, k, sub, :]
                        h_im = spec_h[1, k, sub, :]
                        h_ny = spec_h[2, k, sub, :]
                        sums[2 * a] += x_re * h_re - x_im * h_im
                        sums[2 * a + 1] += x_re * h_im + x_im * h_ny
                return tuple(sums)

            blank = jnp.zeros((half, rows), jnp.float32)
            sums = lax.fori_loop(0, n + 1, add_blocks, (blank,) * (2 * STEP))
            for a in range(STEP):
                spec_y[n * STEP + a, sub, :rows] = sums[2 * a]
                spec_y[n * STEP + a, sub, rows:] = sums[2 * a + 1]
        return 0

    lax.fori_loop(0, n_ctx // STEP, convolve, 0)
    loads[4].wait()

    def restore(n, _):
        at = pl.ds(pl.multiple_of(n * STEP, STEP), STEP)
        wave = spec_y[at].reshape(STEP * cpd, 2 * rows)
        high = wave.astype(jnp.bfloat16)
        low = (wave - high.astype(jnp.float32)).astype(jnp.bfloat16)
        time = (
            jnp.dot(high, inv[0], preferred_element_type=jnp.float32)
            + jnp.dot(low, inv[0], preferred_element_type=jnp.float32)
            + jnp.dot(high, inv[1], preferred_element_type=jnp.float32)
        ).reshape(STEP, cpd, 2 * rows)
        late = time[:, :, rows:]
        before = jnp.concatenate([tail[...], late[: STEP - 1]], axis=0)
        tail[...] = late[STEP - 1 :]
        direct = skip[None] * normed[at].astype(jnp.float32)
        back_out[at] = (time[:, :, :rows] + before + direct).astype(jnp.bfloat16)
        return 0

    lax.fori_loop(0, n_ctx // STEP, restore, 0)
    over_ctx(lambda peer: back_copy(peer, me).start())
    back_in[pl.ds(me, 1)] = back_out[pl.ds(me, 1)]
    loads[3].wait()
    over_ctx(lambda peer: back_copy(peer, peer).wait_recv())
    result = back_in[...].reshape(chans, rows).astype(jnp.float32).T
    out_ref[...] = (gate[...].astype(jnp.float32) * result).astype(jnp.bfloat16)

    over_ch(lambda peer: part_copy(peer, me_ch).wait_send())
    over_ctx(lambda peer: bulk_copy(peer, me).wait_send())
    over_ctx(lambda peer: power_copy(peer, me).wait_send())
    over_ctx(lambda peer: back_copy(peer, me).wait_send())


def solution(mesh):
    n_ctx, n_ch = mesh.shape["ctx"], mesh.shape["ch"]

    def local(signal, norm_gain, skip_gain, filter_taps, out_gate):
        rows, chans = signal.shape
        cpd = chans // n_ctx
        fwd, inv = (jnp.asarray(table) for table in dft_tables(rows))
        f32, bf16 = jnp.float32, jnp.bfloat16
        vmem, dma = pltpu.VMEM, pltpu.SemaphoreType.DMA
        anywhere = pl.BlockSpec(memory_space=pltpu.HBM)
        in_vmem = pl.BlockSpec(memory_space=pltpu.VMEM)
        return pl.pallas_call(
            functools.partial(kernel, n_ctx, n_ch, chans * n_ch),
            out_shape=jax.ShapeDtypeStruct((rows, chans), bf16),
            in_specs=[anywhere] * 3 + [in_vmem] * 2 + [anywhere] * 2,
            out_specs=in_vmem,
            scratch_shapes=[
                vmem((rows, chans), bf16), vmem((rows, chans), bf16), vmem((rows, chans), bf16),
                vmem((2 * rows, 2 * rows), bf16), vmem((2, 2 * rows, 2 * rows), bf16), dma((5,)),
                vmem((n_ctx, 2, cpd, rows), bf16), vmem((n_ctx, 2, cpd, rows), bf16), dma((n_ctx,)), dma((n_ctx,)),
                vmem((n_ch, 1, rows), f32), dma((n_ch,)), dma((n_ch,)),
                vmem((n_ctx, 1, rows), f32), dma((n_ctx,)), dma((n_ctx,)),
                vmem((2, 128, rows), f32), vmem((n_ctx, cpd, rows), bf16),
                vmem((2, n_ctx, cpd, rows), f32), vmem((3, n_ctx + STEP, cpd, rows), f32),
                vmem((n_ctx, cpd, 2 * rows), f32), vmem((1, cpd, rows), f32),
                vmem((n_ctx, cpd, rows), bf16), vmem((n_ctx, cpd, rows), bf16), dma((n_ctx,)), dma((n_ctx,)),
            ],
            compiler_params=pltpu.CompilerParams(
                collective_id=0, has_side_effects=True, vmem_limit_bytes=62 * 1024 * 1024
            ),
        )(signal, filter_taps, out_gate, norm_gain.reshape(-1, 128), skip_gain.reshape(-1, 128), fwd, inv)

    return jax.shard_map(
        local,
        mesh=mesh,
        in_specs=(P("ctx", "ch"), P("ch"), P("ch"), P("ctx", "ch"), P("ctx", "ch")),
        out_specs=P("ctx", "ch"),
        check_vma=False,
    )
```

time: 467 us -> 55.7 us (0.12)
  the two profiles are of different devices: /device:TPU:487 before, /device:TPU:1 now
where the time goes in v1:
time: 55.7 us; the launch traced here: 55.6 us
  Pallas kernels  54 us (97%)
  local copies, waits for them, and re-layouts  1.57 us (3%)
    pallas_call x1, Pallas kernels, local(): pl.pallas_call(functools.partial(kernel, n_ctx, n_ch, chans * n_ch), out_...  54 us
    unnamed x1, local copies, waits for them, and re-layouts  1.57 us

profile of v1, /device:TPU:1, one launch (start us, length us, event | category | flops | bytes accessed | tf_op | source)
XLA Modules:
  0.0 55.6 jit_solution(16576669747704334706)
XLA Ops:
  0.0 54.0 %shard_map.73 = bf16[128,512]{1,0:T(8,128)(2,1)} custom-call(bf16[128,512]{1,0:T(8,128)(2,1)} %sig_hbm.1, bf16[128,512]{1,0:T(8,128)(2,1)} %tap_hbm.1, bf16[128,512]{1,0:T(8,128)(2,1)} %gate_hbm.1, f32[4,128]{1,0:T(4,128)} %bitcast.2, f32[4,128]{1,0:T(4,128)} %bitcast.3, bf16[256,256]{1,0:T(8,128)(2,1)} %constant.4.clone.fwd_hbm, ...), custom_call_target="tpu_custom_call" | custom-call | tf_op jit(solution)/shard_map/pallas_call | solution.py:250
  54.0 1.6 %copy.9 = bf16[128,512]{1,0:T(8,128)(2,1)} copy(bf16[128,512]{1,0:T(8,128)(2,1)} %shard_map.73) | data formatting | bytes 262144

commit v2 on v1

v2 whole, which is shorter than its diff:
```python
import functools
import math

import jax
import jax.numpy as jnp
import ml_dtypes
import numpy as np
from jax import lax
from jax.experimental import pallas as pl
from jax.experimental.pallas import tpu as pltpu
from jax.sharding import PartitionSpec as P

C = 8192
EPS = 1e-06
MESH = pl.DeviceIdType.MESH
STEP = 4


def high_low(table):
    high = table.astype(ml_dtypes.bfloat16)
    low = (table - high.astype(np.float64)).astype(ml_dtypes.bfloat16)
    return high, low


def dft_tables(rows):
    span = 2 * rows
    freq = np.arange(rows)

    def phase(a, b):
        return (a[:, None] * b[None, :] % span) * (2.0 * math.pi / span)

    row = np.arange(rows)
    angle = phase(row, freq)
    fwd_im = -np.sin(angle)
    fwd_im[:, 0] = np.cos(math.pi * row)
    forward = np.concatenate([np.cos(angle), fwd_im], axis=1)
    out = np.arange(span)
    angle = phase(freq, out)
    inv_re = 2.0 * np.cos(angle) / span
    inv_re[0] = 1.0 / span
    inv_im = -2.0 * np.sin(angle) / span
    inv_im[0] = np.cos(math.pi * out) / span
    high, low = high_low(np.concatenate([inv_re, inv_im], axis=0))
    return np.concatenate(high_low(forward), axis=0), np.concatenate([high, high, low], axis=0)


def kernel(
    n_ctx, n_ch, channels_all,
    sig_hbm, tap_hbm, gate_hbm, gain_hbm, skip_hbm, fwd_hbm, inv_hbm, out_ref,
    sig, tap, gate, gain, skip, fwd, inv, load_sem,
    part, part_send, part_recv,
    tap_out, tap_in, x_out, x_in, back_out, back_in, send_sem, recv_sem,
    normed, spec_x, spec_h, spec_y,
):
    rows, chans = sig.shape
    cpd = chans // n_ctx
    half = cpd // 2
    me = lax.axis_index("ctx")
    me_ch = lax.axis_index("ch")

    loads = [
        pltpu.make_async_copy(src, dst, load_sem.at[k])
        for k, (src, dst) in enumerate(
            (
                (sig_hbm, sig), (tap_hbm, tap), (gain_hbm, gain), (fwd_hbm, fwd),
                (inv_hbm, inv), (gate_hbm, gate), (skip_hbm, skip),
            )
        )
    ]
    for load in loads:
        load.start()

    barrier = pltpu.get_barrier_semaphore()

    def ctx_peer(n):
        far = n_ctx // 2 - n // 2
        return lax.rem(jnp.where(n % 2 == 0, me + far, me + n_ctx - far), n_ctx)

    def over_ctx(action):
        def step(n, _):
            action(ctx_peer(n))
            return 0

        lax.fori_loop(1, n_ctx, step, 0)

    def over_ch(action):
        def step(d, _):
            action(lax.rem(me_ch + d, n_ch))
            return 0

        lax.fori_loop(1, n_ch, step, 0)

    def part_copy(peer, slot):
        return pltpu.make_async_remote_copy(
            src_ref=part.at[me_ch], dst_ref=part.at[slot], send_sem=part_send.at[peer], recv_sem=part_recv.at[slot],
            device_id={"ch": peer}, device_id_type=MESH,
        )

    def tile_copy(source, target, k, peer):
        return pltpu.make_async_remote_copy(
            src_ref=source.at[peer], dst_ref=target.at[me], send_sem=send_sem.at[k], recv_sem=recv_sem.at[k],
            device_id={"ctx": peer}, device_id_type=MESH,
        )

    def all_tiles(source, target, k):
        return pltpu.make_async_remote_copy(
            src_ref=source.at[pl.ds(0, n_ctx - 1)], dst_ref=target.at[pl.ds(0, n_ctx - 1)],
            send_sem=send_sem.at[k], recv_sem=recv_sem.at[k],
            device_id={"ctx": ctx_peer(1)}, device_id_type=MESH,
        )

    over_ctx(lambda peer: pl.semaphore_signal(barrier, inc=1, device_id={"ctx": peer}, device_id_type=MESH))
    over_ch(lambda peer: pl.semaphore_signal(barrier, inc=1, device_id={"ch": peer}, device_id_type=MESH))

    loads[0].wait()
    values = sig[...].astype(jnp.float32)
    squares = values * values
    lanes = squares[:, :128]
    for k in range(1, chans // 128):
        lanes += squares[:, k * 128 : (k + 1) * 128]
    part[pl.ds(me_ch, 1)] = jnp.sum(lanes.T, axis=0, keepdims=True).reshape(1, 1, rows)
    loads[1].wait()
    tap_out[...] = tap[...].astype(jnp.float32).T.astype(jnp.bfloat16).reshape(n_ctx, cpd, rows)

    pl.semaphore_wait(barrier, n_ctx + n_ch - 2)
    over_ch(lambda peer: part_copy(peer, me_ch).start())
    over_ctx(lambda peer: tile_copy(tap_out, tap_in, 0, peer).start())
    tap_in[pl.ds(me, 1)] = tap_out[pl.ds(me, 1)]

    loads[2].wait()
    over_ch(lambda peer: part_copy(peer, peer).wait_recv())
    total = jnp.sum(part[...], axis=0)
    scale = jnp.broadcast_to(lax.rsqrt(total / channels_all + EPS), (128, rows)).T
    for k in range(chans // 128):
        at = pl.ds(k * 128, 128)
        normed[:, at] = (sig[:, at].astype(jnp.float32) * scale * gain[:, at]).astype(jnp.bfloat16)
    x_out[...] = normed[...].astype(jnp.float32).T.astype(jnp.bfloat16).reshape(n_ctx, cpd, rows)
    over_ctx(lambda peer: tile_copy(x_out, x_in, 1, peer).start())
    x_in[pl.ds(me, 1)] = x_out[pl.ds(me, 1)]

    def spectrum(tiles):
        lines = tiles.reshape(n_ctx * cpd, rows)
        both = jnp.concatenate([lines, lines], axis=1)
        return jnp.dot(both, fwd[...], preferred_element_type=jnp.float32).reshape(n_ctx, cpd, 2 * rows)

    lane = lax.broadcasted_iota(jnp.int32, (1, 1, rows), 2)
    spec_h[:, :STEP] = jnp.zeros((3, STEP, cpd, rows), jnp.float32)
    loads[3].wait()
    all_tiles(tap_out, tap_in, 0).wait_recv()
    filters = spectrum(tap_in[...])
    h_re, h_im = filters[:, :, :rows], filters[:, :, rows:]
    spec_h[0, STEP:] = h_re
    spec_h[1, STEP:] = jnp.where(lane == 0, 0.0, h_im)
    spec_h[2, STEP:] = jnp.where(lane == 0, h_im, h_re)

    all_tiles(x_out, x_in, 1).wait_recv()
    features = spectrum(x_in[...])
    spec_x[0] = features[:, :, :rows]
    spec_x[1] = features[:, :, rows:]

    def convolve(n, _):
        for part_no in range(2):
            sub = pl.ds(part_no * half, half)

            def add_blocks(m, sums):
                sums = list(sums)
                base = (n - m) * STEP
                for b in range(STEP):
                    x_re = spec_x[0, m * STEP + b, sub, :]
                    x_im = spec_x[1, m * STEP + b, sub, :]
                    for a in range(STEP):
                        k = base + a - b + STEP
                        h_re = spec_h[0, k, sub, :]
                        h_im = spec_h[1, k, sub, :]
                        h_ny = spec_h[2, k, sub, :]
                        sums[2 * a] += x_re * h_re - x_im * h_im
                        sums[2 * a + 1] += x_re * h_im + x_im * h_ny
                return tuple(sums)

            blank = jnp.zeros((half, rows), jnp.float32)
            sums = lax.fori_loop(0, n + 1, add_blocks, (blank,) * (2 * STEP))
            for a in range(STEP):
                spec_y[n * STEP + a, sub, :rows] = sums[2 * a]
                spec_y[n * STEP + a, sub, rows:] = sums[2 * a + 1]
        return 0

    lax.fori_loop(0, n_ctx // STEP, convolve, 0)

    loads[4].wait()
    wave = spec_y[...].reshape(n_ctx * cpd, 2 * rows)
    high = wave.astype(jnp.bfloat16)
    low = (wave - high.astype(jnp.float32)).astype(jnp.bfloat16)
    time = jnp.dot(
        jnp.concatenate([high, low, high], axis=1), inv[...], preferred_element_type=jnp.float32
    ).reshape(n_ctx, cpd, 2 * rows)
    early, late = time[:, :, :rows], time[:, :, rows:]
    back_out[...] = (
        early + jnp.concatenate([jnp.zeros((1, cpd, rows), jnp.float32), late[: n_ctx - 1]], axis=0)
    ).astype(jnp.bfloat16)

    over_ctx(lambda peer: tile_copy(back_out, back_in, 2, peer).start())
    back_in[pl.ds(me, 1)] = back_out[pl.ds(me, 1)]
    loads[5].wait()
    loads[6].wait()
    all_tiles(back_out, back_in, 2).wait_recv()
    result = back_in[...].reshape(chans, rows).astype(jnp.float32).T
    direct = skip[...] * normed[...].astype(jnp.float32)
    out_ref[...] = (gate[...].astype(jnp.float32) * (result + direct)).astype(jnp.bfloat16)

    over_ch(lambda peer: part_copy(peer, me_ch).wait_send())
    all_tiles(tap_out, tap_in, 0).wait_send()
    all_tiles(x_out, x_in, 1).wait_send()
    all_tiles(back_out, back_in, 2).wait_send()


def solution(mesh):
    n_ctx, n_ch = mesh.shape["ctx"], mesh.shape["ch"]

    def local(signal, norm_gain, skip_gain, filter_taps, out_gate):
        rows, chans = signal.shape
        cpd = chans // n_ctx
        fwd, inv = (jnp.asarray(table) for table in dft_tables(rows))
        f32, bf16 = jnp.float32, jnp.bfloat16
        vmem, dma = pltpu.VMEM, pltpu.SemaphoreType.DMA
        hbm = pl.BlockSpec(memory_space=pltpu.HBM)
        block, tiles = vmem((rows, chans), bf16), vmem((n_ctx, cpd, rows), bf16)
        return pl.pallas_call(
            functools.partial(kernel, n_ctx, n_ch, chans * n_ch),
            out_shape=jax.ShapeDtypeStruct((rows, chans), bf16),
            in_specs=[hbm] * 7,
            out_specs=pl.BlockSpec(memory_space=pltpu.VMEM),
            scratch_shapes=[
                block, block, block, vmem((1, chans), f32), vmem((1, chans), f32),
                vmem(fwd.shape, bf16), vmem(inv.shape, bf16), dma((7,)),
                vmem((n_ch, 1, rows), f32), dma((n_ch,)), dma((n_ch,)),
                tiles, tiles, tiles, tiles, tiles, tiles, dma((3,)), dma((3,)),
                block, vmem((2, n_ctx, cpd, rows), f32), vmem((3, n_ctx + STEP, cpd, rows), f32),
                vmem((n_ctx, cpd, 2 * rows), f32),
            ],
            compiler_params=pltpu.CompilerParams(
                collective_id=0, has_side_effects=True, vmem_limit_bytes=62 * 1024 * 1024
            ),
        )(signal, filter_taps, out_gate, norm_gain.reshape(1, -1), skip_gain.reshape(1, -1), fwd, inv)

    return jax.shard_map(
        local,
        mesh=mesh,
        in_specs=(P("ctx", "ch"), P("ch"), P("ch"), P("ctx", "ch"), P("ctx", "ch")),
        out_specs=P("ctx", "ch"),
        check_vma=False,
    )
```

time: 55.7 us -> 45.5 us (0.82)
  Pallas kernels: 54 us -> 43.8 us
    pallas_call x1, Pallas kernels: 54 us -> 43.8 us  [local(): pl.pallas_call(functools.partial(kernel, n_ctx, n_ch, chans * n_ch), out_...]
where the time goes in v2:
time: 45.5 us; the launch traced here: 45.4 us
  Pallas kernels  43.8 us (96%)
  local copies, waits for them, and re-layouts  1.57 us (3%)
    pallas_call x1, Pallas kernels, local(): pl.pallas_call(functools.partial(kernel, n_ctx, n_ch, chans * n_ch), out_...  43.8 us
    unnamed x1, local copies, waits for them, and re-layouts  1.57 us

profile of v2, /device:TPU:1, one launch (start us, length us, event | category | flops | bytes accessed | tf_op | source)
XLA Modules:
  0.0 45.4 jit_solution(9243990221226686235)
XLA Ops:
  0.0 43.8 %shard_map.73 = bf16[128,512]{1,0:T(8,128)(2,1)} custom-call(bf16[128,512]{1,0:T(8,128)(2,1)} %sig_hbm.1, bf16[128,512]{1,0:T(8,128)(2,1)} %tap_hbm.1, bf16[128,512]{1,0:T(8,128)(2,1)} %gate_hbm.1, f32[1,512]{1,0:T(1,128)} %bitcast.2, f32[1,512]{1,0:T(1,128)} %bitcast.3, bf16[256,256]{1,0:T(8,128)(2,1)} %constant.4.clone.fwd_hbm, ...), custom_call_target="tpu_custom_call" | custom-call | tf_op jit(solution)/shard_map/pallas_call | solution.py:227
  43.8 1.6 %copy.9 = bf16[128,512]{1,0:T(8,128)(2,1)} copy(bf16[128,512]{1,0:T(8,128)(2,1)} %shard_map.73) | data formatting | bytes 262144

commit v3 on v2

--- a/solution.py
+++ b/solution.py
@@ -49,14 +49,17 @@
     sig_hbm, tap_hbm, gate_hbm, gain_hbm, skip_hbm, fwd_hbm, inv_hbm, out_ref,
     sig, tap, gate, gain, skip, fwd, inv, load_sem,
     part, part_send, part_recv,
-    tap_out, tap_in, x_out, x_in, back_out, back_in, send_sem, recv_sem,
+    tap_out, tap_relay, tap_in, x_out, x_in, back_out, back_in,
+    send_sem, recv_sem, relay_send, relay_recv, pass_send, far_sem,
     normed, spec_x, spec_h, spec_y,
 ):
     rows, chans = sig.shape
     cpd = chans // n_ctx
-    half = cpd // 2
     me = lax.axis_index("ctx")
     me_ch = lax.axis_index("ch")
+    chip, core, n_chips = me // 2, lax.rem(me, 2), n_ctx // 2
+    reach, turn = n_chips // 4, n_chips // 2
+    relayed = 2 * (turn - reach) - 1
 
     loads = [
         pltpu.make_async_copy(src, dst, load_sem.at[k])
@@ -67,21 +70,28 @@
             )
         )
     ]
-    for load in loads:
-        load.start()
 
     barrier = pltpu.get_barrier_semaphore()
 
-    def ctx_peer(n):
-        far = n_ctx // 2 - n // 2
-        return lax.rem(jnp.where(n % 2 == 0, me + far, me + n_ctx - far), n_ctx)
+    def chip_away(far, right):
+        return lax.rem(jnp.where(right, chip + far, chip + n_chips - far), n_chips)
 
     def over_ctx(action):
         def step(n, _):
-            action(ctx_peer(n))
+            q = n // 2
+            peer_chip = chip_away(turn - (q + 1) // 2, q % 2 == 1)
+            action(2 * peer_chip + jnp.where(n < n_ctx - 2, n % 2, 1 - core))
             return 0
 
-        lax.fori_loop(1, n_ctx, step, 0)
+        lax.fori_loop(0, n_ctx - 1, step, 0)
+
+    def over_near(action):
+        def step(n, _):
+            peer_chip = chip_away(reach - n // 4, (n // 2) % 2 == 1)
+            action(2 * peer_chip + jnp.where(n < 4 * reach, n % 2, 1 - core))
+            return 0
+
+        lax.fori_loop(0, 4 * reach + 1, step, 0)
 
     def over_ch(action):
         def step(d, _):
@@ -102,15 +112,52 @@
             device_id={"ctx": peer}, device_id_type=MESH,
         )
 
-    def all_tiles(source, target, k):
+    def tiles_of(target, count, k):
         return pltpu.make_async_remote_copy(
-            src_ref=source.at[pl.ds(0, n_ctx - 1)], dst_ref=target.at[pl.ds(0, n_ctx - 1)],
+            src_ref=target.at[pl.ds(0, count)], dst_ref=target.at[pl.ds(0, count)],
             send_sem=send_sem.at[k], recv_sem=recv_sem.at[k],
-            device_id={"ctx": ctx_peer(1)}, device_id_type=MESH,
-        )
-
-    over_ctx(lambda peer: pl.semaphore_signal(barrier, inc=1, device_id={"ctx": peer}, device_id_type=MESH))
+            device_id={"ctx": lax.rem(me + 1, n_ctx)}, device_id_type=MESH,
+        )
+
+    def relay_copy(source, relay, k, side):
+        far_first = 2 * chip_away(reach + 1, True) if side == 0 else 2 * chip_away(turn, False) + 1
+        return pltpu.make_async_remote_copy(
+            src_ref=source.at[pl.ds(far_first, relayed)], dst_ref=relay.at[side],
+            send_sem=relay_send.at[side], recv_sem=relay_recv.at[side],
+            device_id={"ctx": 2 * chip_away(reach, side == 0) + core}, device_id_type=MESH,
+        )
+
+    def pass_on(relay, target, k, side, action):
+        origin = 2 * chip_away(reach, side == 1) + core
+        far_first = 2 * (chip + 1) if side == 0 else 2 * (chip + n_chips + reach - turn) + 1
+
+        def step(t, _):
+            action(
+                pltpu.make_async_remote_copy(
+                    src_ref=relay.at[side, t], dst_ref=target.at[origin],
+                    send_sem=pass_send, recv_sem=recv_sem.at[k],
+                    device_id={"ctx": lax.rem(far_first + t, n_ctx)}, device_id_type=MESH,
+                )
+            )
+            return 0
+
+        lax.fori_loop(0, relayed, step, 0)
+
+    def send_tiles(source, relay, target, k):
+        for side in range(2):
+            relay_copy(source, relay, k, side).start()
+        over_near(lambda peer: tile_copy(source, target, k, peer).start())
+        target[pl.ds(me, 1)] = source[pl.ds(me, 1)]
+
+    def forward_tiles(source, relay, target, k):
+        for side in range(2):
+            relay_copy(source, relay, k, side).wait_recv()
+            pass_on(relay, target, k, side, lambda copy: copy.start())
+
+    over_near(lambda peer: pl.semaphore_signal(barrier, inc=1, device_id={"ctx": peer}, device_id_type=MESH))
     over_ch(lambda peer: pl.semaphore_signal(barrier, inc=1, device_id={"ch": peer}, device_id_type=MESH))
+    for load in loads:
+        load.start()
 
     loads[0].wait()
     values = sig[...].astype(jnp.float32)
@@ -120,12 +167,17 @@
         lanes += squares[:, k * 128 : (k + 1) * 128]
     part[pl.ds(me_ch, 1)] = jnp.sum(lanes.T, axis=0, keepdims=True).reshape(1, 1, rows)
     loads[1].wait()
-    tap_out[...] = tap[...].astype(jnp.float32).T.astype(jnp.bfloat16).reshape(n_ctx, cpd, rows)
-
-    pl.semaphore_wait(barrier, n_ctx + n_ch - 2)
+    tap_tiles = tap[...].astype(jnp.float32).T.astype(jnp.bfloat16).reshape(n_ctx, cpd, rows)
+    tap_out[:n_ctx] = tap_tiles
+    tap_out[n_ctx:] = tap_tiles
+
+    pl.semaphore_wait(barrier, 4 * reach + 1 + n_ch - 1)
+    for right in (True, False):
+        pl.semaphore_signal(
+            far_sem, inc=1, device_id={"ctx": 2 * chip_away(reach, right) + core}, device_id_type=MESH
+        )
     over_ch(lambda peer: part_copy(peer, me_ch).start())
-    over_ctx(lambda peer: tile_copy(tap_out, tap_in, 0, peer).start())
-    tap_in[pl.ds(me, 1)] = tap_out[pl.ds(me, 1)]
+    send_tiles(tap_out, tap_relay, tap_in, 0)
 
     loads[2].wait()
     over_ch(lambda peer: part_copy(peer, peer).wait_recv())
@@ -134,54 +186,52 @@
     for k in range(chans // 128):
         at = pl.ds(k * 128, 128)
         normed[:, at] = (sig[:, at].astype(jnp.float32) * scale * gain[:, at]).astype(jnp.bfloat16)
-    x_out[...] = normed[...].astype(jnp.float32).T.astype(jnp.bfloat16).reshape(n_ctx, cpd, rows)
+    x_tiles = normed[...].astype(jnp.float32).T.astype(jnp.bfloat16).reshape(n_ctx, cpd, rows)
+    x_out[...] = x_tiles
+    pl.semaphore_wait(far_sem, 2)
     over_ctx(lambda peer: tile_copy(x_out, x_in, 1, peer).start())
     x_in[pl.ds(me, 1)] = x_out[pl.ds(me, 1)]
+    forward_tiles(tap_out, tap_relay, tap_in, 0)
 
     def spectrum(tiles):
         lines = tiles.reshape(n_ctx * cpd, rows)
         both = jnp.concatenate([lines, lines], axis=1)
         return jnp.dot(both, fwd[...], preferred_element_type=jnp.float32).reshape(n_ctx, cpd, 2 * rows)
 
-    lane = lax.broadcasted_iota(jnp.int32, (1, 1, rows), 2)
     spec_h[:, :STEP] = jnp.zeros((3, STEP, cpd, rows), jnp.float32)
     loads[3].wait()
-    all_tiles(tap_out, tap_in, 0).wait_recv()
-    filters = spectrum(tap_in[...])
-    h_re, h_im = filters[:, :, :rows], filters[:, :, rows:]
-    spec_h[0, STEP:] = h_re
-    spec_h[1, STEP:] = jnp.where(lane == 0, 0.0, h_im)
-    spec_h[2, STEP:] = jnp.where(lane == 0, h_im, h_re)
-
-    all_tiles(x_out, x_in, 1).wait_recv()
-    features = spectrum(x_in[...])
-    spec_x[0] = features[:, :, :rows]
-    spec_x[1] = features[:, :, rows:]
+
+    def keep_spectrum(tiles, spec, first):
+        whole = spectrum(tiles)
+        re, im = whole[:, :, :rows], whole[:, :, rows:]
+        spec[0, first:] = re
+        spec[1, first:] = im
+        spec[2, first:] = re + im
+
+    tiles_of(tap_in, n_ctx - 1, 0).wait_recv()
+    keep_spectrum(tap_in[...], spec_h, STEP)
+    tiles_of(x_in, n_ctx - 1, 1).wait_recv()
+    keep_spectrum(x_in[...], spec_x, 0)
+
+    lane = lax.broadcasted_iota(jnp.int32, (cpd, rows), 1)
 
     def convolve(n, _):
-        for part_no in range(2):
-            sub = pl.ds(part_no * half, half)
-
-            def add_blocks(m, sums):
-                sums = list(sums)
-                base = (n - m) * STEP
-                for b in range(STEP):
-                    x_re = spec_x[0, m * STEP + b, sub, :]
-                    x_im = spec_x[1, m * STEP + b, sub, :]
-                    for a in range(STEP):
-                        k = base + a - b + STEP
-                        h_re = spec_h[0, k, sub, :]
-                        h_im = spec_h[1, k, sub, :]
-                        h_ny = spec_h[2, k, sub, :]
-                        sums[2 * a] += x_re * h_re - x_im * h_im
-                        sums[2 * a + 1] += x_re * h_im + x_im * h_ny
-                return tuple(sums)
-
-            blank = jnp.zeros((half, rows), jnp.float32)
-            sums = lax.fori_loop(0, n + 1, add_blocks, (blank,) * (2 * STEP))
-            for a in range(STEP):
-                spec_y[n * STEP + a, sub, :rows] = sums[2 * a]
-                spec_y[n * STEP + a, sub, rows:] = sums[2 * a + 1]
+        def add_blocks(m, sums):
+            sums = list(sums)
+            base = (n - m) * STEP
+            for b in range(STEP):
+                x = [spec_x[k, m * STEP + b] for k in range(3)]
+                for a in range(STEP):
+                    for k in range(3):
+                        sums[3 * a + k] += x[k] * spec_h[k, base + a - b + STEP]
+            return tuple(sums)
+
+        blank = jnp.zeros((cpd, rows), jnp.float32)
+        sums = lax.fori_loop(0, n + 1, add_blocks, (blank,) * (3 * STEP))
+        for a in range(STEP):
+            re, im, both = sums[3 * a : 3 * a + 3]
+            spec_y[n * STEP + a, :, :rows] = jnp.where(lane == 0, re, re - im)
+            spec_y[n * STEP + a, :, rows:] = jnp.where(lane == 0, im, both - re - im)
         return 0
 
     lax.fori_loop(0, n_ctx // STEP, convolve, 0)
@@ -202,15 +252,18 @@
     back_in[pl.ds(me, 1)] = back_out[pl.ds(me, 1)]
     loads[5].wait()
     loads[6].wait()
-    all_tiles(back_out, back_in, 2).wait_recv()
+    direct = skip[...] * normed[...].astype(jnp.float32)
+    tiles_of(back_in, n_ctx - 1, 2).wait_recv()
     result = back_in[...].reshape(chans, rows).astype(jnp.float32).T
-    direct = skip[...] * normed[...].astype(jnp.float32)
     out_ref[...] = (gate[...].astype(jnp.float32) * (result + direct)).astype(jnp.bfloat16)
 
     over_ch(lambda peer: part_copy(peer, me_ch).wait_send())
-    all_tiles(tap_out, tap_in, 0).wait_send()
-    all_tiles(x_out, x_in, 1).wait_send()
-    all_tiles(back_out, back_in, 2).wait_send()
+    tiles_of(tap_in, 4 * reach + 1, 0).wait_send()
+    for side in range(2):
+        relay_copy(tap_out, tap_relay, 0, side).wait_send()
+        pass_on(tap_relay, tap_in, 0, side, lambda copy: copy.wait_send())
+    tiles_of(x_in, n_ctx - 1, 1).wait_send()
+    tiles_of(back_in, n_ctx - 1, 2).wait_send()
 
 
 def solution(mesh):
@@ -224,6 +277,8 @@
         vmem, dma = pltpu.VMEM, pltpu.SemaphoreType.DMA
         hbm = pl.BlockSpec(memory_space=pltpu.HBM)
         block, tiles = vmem((rows, chans), bf16), vmem((n_ctx, cpd, rows), bf16)
+        twice = vmem((2 * n_ctx, cpd, rows), bf16)
+        relay = vmem((2, 2 * (n_ctx // 4 - n_ctx // 8) - 1, cpd, rows), bf16)
         return pl.pallas_call(
             functools.partial(kernel, n_ctx, n_ch, chans * n_ch),
             out_shape=jax.ShapeDtypeStruct((rows, chans), bf16),
@@ -233,8 +288,9 @@
                 block, block, block, vmem((1, chans), f32), vmem((1, chans), f32),
                 vmem(fwd.shape, bf16), vmem(inv.shape, bf16), dma((7,)),
                 vmem((n_ch, 1, rows), f32), dma((n_ch,)), dma((n_ch,)),
-                tiles, tiles, tiles, tiles, tiles, tiles, dma((3,)), dma((3,)),
-                block, vmem((2, n_ctx, cpd, rows), f32), vmem((3, n_ctx + STEP, cpd, rows), f32),
+                twice, relay, tiles, tiles, tiles, tiles, tiles,
+                dma((3,)), dma((3,)), dma((2,)), dma((2,)), dma(()), pltpu.SemaphoreType.REGULAR,
+                block, vmem((3, n_ctx, cpd, rows), f32), vmem((3, n_ctx + STEP, cpd, rows), f32),
                 vmem((n_ctx, cpd, 2 * rows), f32),
             ],
             compiler_params=pltpu.CompilerParams(

time: 45.5 us -> 44.9 us (0.987)
  Pallas kernels: 43.8 us -> 43.2 us
    pallas_call x1, Pallas kernels: 43.8 us -> 43.2 us  [local(): pl.pallas_call(functools.partial(kernel, n_ctx, n_ch, chans * n_ch), out_...]
where the time goes in v3:
time: 44.9 us; the launch traced here: 44.8 us
  Pallas kernels  43.2 us (96%)
  local copies, waits for them, and re-layouts  1.57 us (3%)
    pallas_call x1, Pallas kernels, local(): pl.pallas_call(functools.partial(kernel, n_ctx, n_ch, chans * n_ch), out_...  43.2 us
    unnamed x1, local copies, waits for them, and re-layouts  1.57 us

profile of v3, /device:TPU:1, one launch (start us, length us, event | category | flops | bytes accessed | tf_op | source)
XLA Modules:
  0.0 44.8 jit_solution(9603792534115902311)
XLA Ops:
  0.0 43.2 %shard_map.73 = bf16[128,512]{1,0:T(8,128)(2,1)} custom-call(bf16[128,512]{1,0:T(8,128)(2,1)} %sig_hbm.1, bf16[128,512]{1,0:T(8,128)(2,1)} %tap_hbm.1, bf16[128,512]{1,0:T(8,128)(2,1)} %gate_hbm.1, f32[1,512]{1,0:T(1,128)} %bitcast.2, f32[1,512]{1,0:T(1,128)} %bitcast.3, bf16[256,256]{1,0:T(8,128)(2,1)} %constant.4.clone.fwd_hbm, ...), custom_call_target="tpu_custom_call" | custom-call | tf_op jit(solution)/shard_map/pallas_call | solution.py:282
  43.2 1.6 %copy.9 = bf16[128,512]{1,0:T(8,128)(2,1)} copy(bf16[128,512]{1,0:T(8,128)(2,1)} %shard_map.73) | data formatting | bytes 262144

commit v4 on v3

--- a/solution.py
+++ b/solution.py
@@ -13,7 +13,7 @@
 C = 8192
 EPS = 1e-06
 MESH = pl.DeviceIdType.MESH
-STEP = 4
+STEP = 8
 
 
 def high_low(table):
@@ -55,6 +55,7 @@
 ):
     rows, chans = sig.shape
     cpd = chans // n_ctx
+    half = cpd // 2
     me = lax.axis_index("ctx")
     me_ch = lax.axis_index("ch")
     chip, core, n_chips = me // 2, lax.rem(me, 2), n_ctx // 2
@@ -111,6 +112,15 @@
             src_ref=source.at[peer], dst_ref=target.at[me], send_sem=send_sem.at[k], recv_sem=recv_sem.at[k],
             device_id={"ctx": peer}, device_id_type=MESH,
         )
+
+    def half_copy(source, target, k, peer):
+        return pltpu.make_async_remote_copy(
+            src_ref=source, dst_ref=target, send_sem=send_sem.at[k], recv_sem=recv_sem.at[k],
+            device_id={"ctx": peer}, device_id_type=MESH,
+        )
+
+    def halves_of(source, target, k):
+        return half_copy(source, target, k, lax.rem(me + 1, n_ctx))
 
     def tiles_of(target, count, k):
         return pltpu.make_async_remote_copy(
@@ -186,75 +196,77 @@
     for k in range(chans // 128):
         at = pl.ds(k * 128, 128)
         normed[:, at] = (sig[:, at].astype(jnp.float32) * scale * gain[:, at]).astype(jnp.bfloat16)
-    x_tiles = normed[...].astype(jnp.float32).T.astype(jnp.bfloat16).reshape(n_ctx, cpd, rows)
-    x_out[...] = x_tiles
+    x_tiles = normed[...].astype(jnp.float32).T.reshape(n_ctx, 2, half, rows)
+    x_out[...] = x_tiles.astype(jnp.bfloat16)
     pl.semaphore_wait(far_sem, 2)
-    over_ctx(lambda peer: tile_copy(x_out, x_in, 1, peer).start())
-    x_in[pl.ds(me, 1)] = x_out[pl.ds(me, 1)]
+    for part_no in range(2):
+        over_ctx(lambda peer: half_copy(x_out.at[peer, part_no], x_in.at[part_no, me], 1 + part_no, peer).start())
+        x_in[part_no, pl.ds(me, 1)] = x_out[pl.ds(me, 1), part_no]
     forward_tiles(tap_out, tap_relay, tap_in, 0)
 
     def spectrum(tiles):
-        lines = tiles.reshape(n_ctx * cpd, rows)
+        lines = tiles.reshape(-1, rows)
         both = jnp.concatenate([lines, lines], axis=1)
-        return jnp.dot(both, fwd[...], preferred_element_type=jnp.float32).reshape(n_ctx, cpd, 2 * rows)
+        whole = jnp.dot(both, fwd[...], preferred_element_type=jnp.float32).reshape(n_ctx, -1, 2 * rows)
+        re, im = whole[:, :, :rows], whole[:, :, rows:]
+        return re, im, re + im
 
     spec_h[:, :STEP] = jnp.zeros((3, STEP, cpd, rows), jnp.float32)
     loads[3].wait()
-
-    def keep_spectrum(tiles, spec, first):
-        whole = spectrum(tiles)
-        re, im = whole[:, :, :rows], whole[:, :, rows:]
-        spec[0, first:] = re
-        spec[1, first:] = im
-        spec[2, first:] = re + im
-
     tiles_of(tap_in, n_ctx - 1, 0).wait_recv()
-    keep_spectrum(tap_in[...], spec_h, STEP)
-    tiles_of(x_in, n_ctx - 1, 1).wait_recv()
-    keep_spectrum(x_in[...], spec_x, 0)
-
-    lane = lax.broadcasted_iota(jnp.int32, (cpd, rows), 1)
-
-    def convolve(n, _):
-        def add_blocks(m, sums):
-            sums = list(sums)
-            base = (n - m) * STEP
-            for b in range(STEP):
-                x = [spec_x[k, m * STEP + b] for k in range(3)]
-                for a in range(STEP):
-                    for k in range(3):
-                        sums[3 * a + k] += x[k] * spec_h[k, base + a - b + STEP]
-            return tuple(sums)
-
-        blank = jnp.zeros((cpd, rows), jnp.float32)
-        sums = lax.fori_loop(0, n + 1, add_blocks, (blank,) * (3 * STEP))
-        for a in range(STEP):
-            re, im, both = sums[3 * a : 3 * a + 3]
-            spec_y[n * STEP + a, :, :rows] = jnp.where(lane == 0, re, re - im)
-            spec_y[n * STEP + a, :, rows:] = jnp.where(lane == 0, im, both - re - im)
-        return 0
-
-    lax.fori_loop(0, n_ctx // STEP, convolve, 0)
-
+    for k, values in enumerate(spectrum(tap_in[...])):
+        spec_h[k, STEP:] = values
     loads[4].wait()
-    wave = spec_y[...].reshape(n_ctx * cpd, 2 * rows)
-    high = wave.astype(jnp.bfloat16)
-    low = (wave - high.astype(jnp.float32)).astype(jnp.bfloat16)
-    time = jnp.dot(
-        jnp.concatenate([high, low, high], axis=1), inv[...], preferred_element_type=jnp.float32
-    ).reshape(n_ctx, cpd, 2 * rows)
-    early, late = time[:, :, :rows], time[:, :, rows:]
-    back_out[...] = (
-        early + jnp.concatenate([jnp.zeros((1, cpd, rows), jnp.float32), late[: n_ctx - 1]], axis=0)
-    ).astype(jnp.bfloat16)
-
-    over_ctx(lambda peer: tile_copy(back_out, back_in, 2, peer).start())
-    back_in[pl.ds(me, 1)] = back_out[pl.ds(me, 1)]
+
+    lane = lax.broadcasted_iota(jnp.int32, (half, rows), 1)
+
+    for part_no in range(2):
+        sub = pl.ds(part_no * half, half)
+        halves_of(x_in.at[part_no, pl.ds(0, n_ctx - 1)], x_in.at[part_no, pl.ds(0, n_ctx - 1)], 1 + part_no).wait_recv()
+        lines = x_in[part_no].astype(jnp.float32).reshape(n_ctx * half, rows).astype(jnp.bfloat16)
+        for k, values in enumerate(spectrum(lines)):
+            spec_x[k] = values
+
+        def convolve(n, _):
+            def add_blocks(m, sums):
+                sums = list(sums)
+                base = (n - m) * STEP
+                for b in range(STEP):
+                    x = [spec_x[k, m * STEP + b] for k in range(3)]
+                    for a in range(STEP):
+                        for k in range(3):
+                            sums[3 * a + k] += x[k] * spec_h[k, base + a - b + STEP, sub, :]
+                return tuple(sums)
+
+            blank = jnp.zeros((half, rows), jnp.float32)
+            sums = lax.fori_loop(0, n + 1, add_blocks, (blank,) * (3 * STEP))
+            for a in range(STEP):
+                re, im, both = sums[3 * a : 3 * a + 3]
+                spec_y[n * STEP + a, :, :rows] = jnp.where(lane == 0, re, re - im)
+                spec_y[n * STEP + a, :, rows:] = jnp.where(lane == 0, im, both - re - im)
+            return 0
+
+        lax.fori_loop(0, n_ctx // STEP, convolve, 0)
+        wave = spec_y[...].reshape(n_ctx * half, 2 * rows)
+        high = wave.astype(jnp.bfloat16)
+        low = (wave - high.astype(jnp.float32)).astype(jnp.bfloat16)
+        time = jnp.dot(
+            jnp.concatenate([high, low, high], axis=1), inv[...], preferred_element_type=jnp.float32
+        ).reshape(n_ctx, half, 2 * rows)
+        early, late = time[:, :, :rows], time[:, :, rows:]
+        back_out[part_no] = (
+            early + jnp.concatenate([jnp.zeros((1, half, rows), jnp.float32), late[: n_ctx - 1]], axis=0)
+        ).astype(jnp.bfloat16)
+        over_ctx(lambda peer: half_copy(back_out.at[part_no, peer], back_in.at[me, part_no], 3 + part_no, peer).start())
+        back_in[pl.ds(me, 1), part_no] = back_out[part_no, pl.ds(me, 1)]
+
     loads[5].wait()
     loads[6].wait()
     direct = skip[...] * normed[...].astype(jnp.float32)
-    tiles_of(back_in, n_ctx - 1, 2).wait_recv()
-    result = back_in[...].reshape(chans, rows).astype(jnp.float32).T
+    some_back = back_in.at[pl.ds(0, n_ctx - 1), 0]
+    for part_no in range(2):
+        halves_of(back_out.at[part_no, pl.ds(0, n_ctx - 1)], some_back, 3 + part_no).wait_recv()
+    result = back_in[...].astype(jnp.float32).reshape(chans, rows).T
     out_ref[...] = (gate[...].astype(jnp.float32) * (result + direct)).astype(jnp.bfloat16)
 
     over_ch(lambda peer: part_copy(peer, me_ch).wait_send())
@@ -262,8 +274,9 @@
     for side in range(2):
         relay_copy(tap_out, tap_relay, 0, side).wait_send()
         pass_on(tap_relay, tap_in, 0, side, lambda copy: copy.wait_send())
-    tiles_of(x_in, n_ctx - 1, 1).wait_send()
-    tiles_of(back_in, n_ctx - 1, 2).wait_send()
+    some_x = x_in.at[0, pl.ds(0, n_ctx - 1)]
+    for k in range(1, 5):
+        halves_of(some_x, some_x, k).wait_send()
 
 
 def solution(mesh):
@@ -288,10 +301,11 @@
                 block, block, block, vmem((1, chans), f32), vmem((1, chans), f32),
                 vmem(fwd.shape, bf16), vmem(inv.shape, bf16), dma((7,)),
                 vmem((n_ch, 1, rows), f32), dma((n_ch,)), dma((n_ch,)),
-                twice, relay, tiles, tiles, tiles, tiles, tiles,
-                dma((3,)), dma((3,)), dma((2,)), dma((2,)), dma(()), pltpu.SemaphoreType.REGULAR,
-                block, vmem((3, n_ctx, cpd, rows), f32), vmem((3, n_ctx + STEP, cpd, rows), f32),
-                vmem((n_ctx, cpd, 2 * rows), f32),
+                twice, relay, tiles, vmem((n_ctx, 2, cpd // 2, rows), bf16), vmem((2, n_ctx, cpd // 2, rows), bf16),
+                vmem((2, n_ctx, cpd // 2, rows), bf16), vmem((n_ctx, 2, cpd // 2, rows), bf16),
+                dma((5,)), dma((5,)), dma((2,)), dma((2,)), dma(()), pltpu.SemaphoreType.REGULAR,
+                block, vmem((3, n_ctx, cpd // 2, rows), f32), vmem((3, n_ctx + STEP, cpd, rows), f32),
+                vmem((n_ctx, cpd // 2, 2 * rows), f32),
             ],
             compiler_params=pltpu.CompilerParams(
                 collective_id=0, has_side_effects=True, vmem_limit_bytes=62 * 1024 * 1024

time: 44.9 us -> 44.8 us (level)
  no operation moved by 1% of the time
where the time goes in v4:
time: 44.8 us; the launch traced here: 44.7 us
  Pallas kernels  43.1 us (96%)
  local copies, waits for them, and re-layouts  1.57 us (4%)
    pallas_call x1, Pallas kernels, local(): pl.pallas_call(functools.partial(kernel, n_ctx, n_ch, chans * n_ch), out_...  43.1 us
    unnamed x1, local copies, waits for them, and re-layouts  1.57 us

profile of v4, /device:TPU:1, one launch (start us, length us, event | category | flops | bytes accessed | tf_op | source)
XLA Modules:
  0.0 44.7 jit_solution(8181655403967639680)
XLA Ops:
  0.0 43.1 %shard_map.73 = bf16[128,512]{1,0:T(8,128)(2,1)} custom-call(bf16[128,512]{1,0:T(8,128)(2,1)} %sig_hbm.1, bf16[128,512]{1,0:T(8,128)(2,1)} %tap_hbm.1, bf16[128,512]{1,0:T(8,128)(2,1)} %gate_hbm.1, f32[1,512]{1,0:T(1,128)} %bitcast.2, f32[1,512]{1,0:T(1,128)} %bitcast.3, bf16[256,256]{1,0:T(8,128)(2,1)} %constant.4.clone.fwd_hbm, ...), custom_call_target="tpu_custom_call" | custom-call | tf_op jit(solution)/shard_map/pallas_call | solution.py:295
  43.1 1.6 %copy.9 = bf16[128,512]{1,0:T(8,128)(2,1)} copy(bf16[128,512]{1,0:T(8,128)(2,1)} %shard_map.73) | data formatting | bytes 262144

commit v5 on v4

--- a/solution.py
+++ b/solution.py
@@ -51,7 +51,7 @@
     part, part_send, part_recv,
     tap_out, tap_relay, tap_in, x_out, x_in, back_out, back_in,
     send_sem, recv_sem, relay_send, relay_recv, pass_send, far_sem,
-    normed, spec_x, spec_h, spec_y,
+    normed, turned, spec_x, spec_h, spec_y,
 ):
     rows, chans = sig.shape
     cpd = chans // n_ctx
@@ -190,19 +190,19 @@
     send_tiles(tap_out, tap_relay, tap_in, 0)
 
     loads[2].wait()
+    turned[...] = (values * gain[...]).T
     over_ch(lambda peer: part_copy(peer, peer).wait_recv())
-    total = jnp.sum(part[...], axis=0)
-    scale = jnp.broadcast_to(lax.rsqrt(total / channels_all + EPS), (128, rows)).T
-    for k in range(chans // 128):
-        at = pl.ds(k * 128, 128)
-        normed[:, at] = (sig[:, at].astype(jnp.float32) * scale * gain[:, at]).astype(jnp.bfloat16)
-    x_tiles = normed[...].astype(jnp.float32).T.reshape(n_ctx, 2, half, rows)
-    x_out[...] = x_tiles.astype(jnp.bfloat16)
+    scale = lax.rsqrt(jnp.sum(part[...], axis=0) / channels_all + EPS)
+    x_out[...] = (turned[...] * scale).reshape(n_ctx, 2, half, rows).astype(jnp.bfloat16)
     pl.semaphore_wait(far_sem, 2)
     for part_no in range(2):
         over_ctx(lambda peer: half_copy(x_out.at[peer, part_no], x_in.at[part_no, me], 1 + part_no, peer).start())
         x_in[part_no, pl.ds(me, 1)] = x_out[pl.ds(me, 1), part_no]
     forward_tiles(tap_out, tap_relay, tap_in, 0)
+    column = jnp.broadcast_to(scale, (128, rows)).T
+    for k in range(chans // 128):
+        at = pl.ds(k * 128, 128)
+        normed[:, at] = (sig[:, at].astype(jnp.float32) * gain[:, at] * column).astype(jnp.bfloat16)
 
     def spectrum(tiles):
         lines = tiles.reshape(-1, rows)
@@ -304,7 +304,7 @@
                 twice, relay, tiles, vmem((n_ctx, 2, cpd // 2, rows), bf16), vmem((2, n_ctx, cpd // 2, rows), bf16),
                 vmem((2, n_ctx, cpd // 2, rows), bf16), vmem((n_ctx, 2, cpd // 2, rows), bf16),
                 dma((5,)), dma((5,)), dma((2,)), dma((2,)), dma(()), pltpu.SemaphoreType.REGULAR,
-                block, vmem((3, n_ctx, cpd // 2, rows), f32), vmem((3, n_ctx + STEP, cpd, rows), f32),
+                block, vmem((chans, rows), f32), vmem((3, n_ctx, cpd // 2, rows), f32), vmem((3, n_ctx + STEP, cpd, rows), f32),
                 vmem((n_ctx, cpd // 2, 2 * rows), f32),
             ],
             compiler_params=pltpu.CompilerParams(

time: 44.8 us -> 44.5 us (level)
  no operation moved by 1% of the time
where the time goes in v5:
time: 44.5 us; the launch traced here: 44.3 us
  Pallas kernels  42.8 us (96%)
  local copies, waits for them, and re-layouts  1.57 us (4%)
    pallas_call x1, Pallas kernels, local(): pl.pallas_call(functools.partial(kernel, n_ctx, n_ch, chans * n_ch), out_...  42.8 us
    unnamed x1, local copies, waits for them, and re-layouts  1.57 us

profile of v5, /device:TPU:1, one launch (start us, length us, event | category | flops | bytes accessed | tf_op | source)
XLA Modules:
  0.0 44.3 jit_solution(11121863865889645894)
XLA Ops:
  0.0 42.8 %shard_map.73 = bf16[128,512]{1,0:T(8,128)(2,1)} custom-call(bf16[128,512]{1,0:T(8,128)(2,1)} %sig_hbm.1, bf16[128,512]{1,0:T(8,128)(2,1)} %tap_hbm.1, bf16[128,512]{1,0:T(8,128)(2,1)} %gate_hbm.1, f32[1,512]{1,0:T(1,128)} %bitcast.2, f32[1,512]{1,0:T(1,128)} %bitcast.3, bf16[256,256]{1,0:T(8,128)(2,1)} %constant.4.clone.fwd_hbm, ...), custom_call_target="tpu_custom_call" | custom-call | tf_op jit(solution)/shard_map/pallas_call | solution.py:295
  42.8 1.6 %copy.9 = bf16[128,512]{1,0:T(8,128)(2,1)} copy(bf16[128,512]{1,0:T(8,128)(2,1)} %shard_map.73) | data formatting | bytes 262144

commit v6 on v5

--- a/solution.py
+++ b/solution.py
@@ -263,12 +263,6 @@
     loads[5].wait()
     loads[6].wait()
     direct = skip[...] * normed[...].astype(jnp.float32)
-    some_back = back_in.at[pl.ds(0, n_ctx - 1), 0]
-    for part_no in range(2):
-        halves_of(back_out.at[part_no, pl.ds(0, n_ctx - 1)], some_back, 3 + part_no).wait_recv()
-    result = back_in[...].astype(jnp.float32).reshape(chans, rows).T
-    out_ref[...] = (gate[...].astype(jnp.float32) * (result + direct)).astype(jnp.bfloat16)
-
     over_ch(lambda peer: part_copy(peer, me_ch).wait_send())
     tiles_of(tap_in, 4 * reach + 1, 0).wait_send()
     for side in range(2):
@@ -277,6 +271,11 @@
     some_x = x_in.at[0, pl.ds(0, n_ctx - 1)]
     for k in range(1, 5):
         halves_of(some_x, some_x, k).wait_send()
+    some_back = back_in.at[pl.ds(0, n_ctx - 1), 0]
+    for part_no in range(2):
+        halves_of(back_out.at[part_no, pl.ds(0, n_ctx - 1)], some_back, 3 + part_no).wait_recv()
+    result = back_in[...].astype(jnp.float32).reshape(chans, rows).T
+    out_ref[...] = (gate[...].astype(jnp.float32) * (result + direct)).astype(jnp.bfloat16)
 
 
 def solution(mesh):

time: 44.5 us -> 44.3 us (level)
  no operation moved by 1% of the time
where the time goes in v6:
time: 44.3 us; the launch traced here: 44.1 us
  Pallas kernels  42.5 us (96%)
  local copies, waits for them, and re-layouts  1.57 us (4%)
    pallas_call x1, Pallas kernels, local(): pl.pallas_call(functools.partial(kernel, n_ctx, n_ch, chans * n_ch), out_...  42.5 us
    unnamed x1, local copies, waits for them, and re-layouts  1.57 us

profile of v6, /device:TPU:1, one launch (start us, length us, event | category | flops | bytes accessed | tf_op | source)
XLA Modules:
  0.0 44.1 jit_solution(9109328130308468522)
XLA Ops:
  0.0 42.5 %shard_map.73 = bf16[128,512]{1,0:T(8,128)(2,1)} custom-call(bf16[128,512]{1,0:T(8,128)(2,1)} %sig_hbm.1, bf16[128,512]{1,0:T(8,128)(2,1)} %tap_hbm.1, bf16[128,512]{1,0:T(8,128)(2,1)} %gate_hbm.1, f32[1,512]{1,0:T(1,128)} %bitcast.2, f32[1,512]{1,0:T(1,128)} %bitcast.3, bf16[256,256]{1,0:T(8,128)(2,1)} %constant.4.clone.fwd_hbm, ...), custom_call_target="tpu_custom_call" | custom-call | tf_op jit(solution)/shard_map/pallas_call | solution.py:294
  42.6 1.6 %copy.9 = bf16[128,512]{1,0:T(8,128)(2,1)} copy(bf16[128,512]{1,0:T(8,128)(2,1)} %shard_map.73) | data formatting | bytes 262144
